TPU v7x, 128 devices: a whole 4x4x4 slice. The times are simulated.
128 devices in a mesh: outer: 8 (over z, core), inner: 16 (over y, x).
Axes of the slice: x: 4, y: 4, z: 4, core: 2. Of those that a mesh axis runs over, the one named last changes fastest.
Arguments:
- tokens_in: bfloat16 [16384, 2048], P(('outer', 'inner')), may hold values from -6 to 6
- expert_ids: int32 [16384, 10], P(('outer', 'inner')), may hold values from 0 to 255, all different within a row; in each aligned block of 128 rows (0 to 127, 128 to 255, ...) at most 6 rows name the same one
- route_weight: float32 [16384, 10], P(('outer', 'inner')), may hold values from 0.05 to 1
- first_gain: float32 [2048], replicated, may hold values from 0.5 to 1.5
- gate_weight: bfloat16 [256, 2048, 512], P(('outer', 'inner')), may hold values from -0.125 to 0.125
- up_weight: bfloat16 [256, 2048, 512], P(('outer', 'inner')), may hold values from -0.125 to 0.125
- down_weight: bfloat16 [256, 512, 2048], P(('outer', 'inner')), may hold values from -0.25 to 0.25
- second_gain: float32 [2048], replicated, may hold values from 0.5 to 1.5
- mixer_weight: bfloat16 [2048, 4096], P(None, 'inner'), may hold values from -0.125 to 0.125
- gating_weight: bfloat16 [2048, 32], replicated, may hold values from -0.125 to 0.125
- filter_taps: bfloat16 [4, 4096], replicated, may hold values from -3 to 3
- decay_log: float32 [16], replicated, may hold values from -9 to -3
- decay_bias: float32 [16], replicated, may hold values from -1 to 1
- output_gain: float32 [128], replicated, may hold values from 0.5 to 1.5
Outputs:
- hidden_out: bfloat16 [16384, 2048], P(('outer', 'inner'))
- core_out: bfloat16 [16384, 2048], P(('outer', 'inner'))
Inputs may be any that keep to these rules, and one draw needn't show every extreme that they name: `expert_ids`: each token names 10 different experts; the 128 rows of one device name any one expert at most 6 times, a bound that some block reaches.
All inputs are finite; a program needn't handle non-finite values.
Results may differ from a plain program's by a relative error of at most 0.015.
Values may be sent and summed in bfloat16 or wider, within the bound.
A program may use at most 576 MiB of HBM per device.

v0:
```python
import jax
import jax.numpy as jnp
from jax import lax
from jax.sharding import PartitionSpec as P


def shifted(value, axis, steps):
    count = lax.axis_size(axis)
    leading, last = (max(0, -steps), min(count, count - steps))
    return lax.ppermute(value, axis, [(source, source + steps) for source in range(leading, last)])


def prefix_2(x, axis, join, neutral):
    place = lax.axis_index(axis)
    gathered = jax.tree.map(
        lambda a, kind: lax.all_gather(a.astype(kind), axis), x, (jnp.bfloat16, jnp.bfloat16)
    )
    state = jax.tree.map(lambda a, e: jnp.zeros_like(a) + jnp.asarray(e, a.dtype), x, neutral)

    def one(lap, state):
        return join(
            state,
            jax.tree.map(
                lambda a, own: lax.dynamic_index_in_dim(a, lap, 0, False).astype(own.dtype),
                gathered,
                x,
            ),
        )

    return lax.fori_loop(0, place, one, state)


def shortened(x):

    def short(part):
        return part.astype(jnp.bfloat16) if part.dtype == jnp.float32 else part

    return jax.tree.map(short, x)


def spread_2(value, axis, source):
    kept = jnp.where(lax.axis_index(axis) == source, value, 0).astype(value.dtype)
    return lax.psum(kept, axis)


def entering(x, axis, combine, identity):
    length, place = (lax.axis_size(axis), lax.axis_index(axis))
    everything = jax.tree.map(
        lambda part, kind: lax.all_gather(part.astype(kind), axis),
        x,
        jax.tree.map(lambda a: jnp.bfloat16 if a.dtype == jnp.float32 else a.dtype, x),
    )
    start = jax.tree.map(
        lambda part, zero: jnp.broadcast_to(jnp.asarray(zero, part.dtype), part.shape), x, identity
    )

    def lap(k, before):
        reached = k < place
        new = combine(
            before, jax.tree.map(lambda part, own: part[k].astype(own.dtype), everything, x)
        )
        return jax.tree.map(lambda a, b: jnp.where(reached, a, b), new, before)

    return lax.fori_loop(0, length, lap, start)


def rms_scale(values, gain):
    wide = values.astype(jnp.float32)
    return wide * lax.rsqrt(jnp.mean(wide * wide, axis=-1, keepdims=True) + 1e-06) * gain


def unit_heads(values):
    return values * lax.rsqrt(jnp.sum(values * values, axis=-1, keepdims=True) + 1e-06)


def run_experts(piece, gate_weight, up_weight, down_weight):
    gate = jnp.einsum("esd,edf->esf", piece, gate_weight, preferred_element_type=jnp.float32)
    upper = jnp.einsum("esd,edf->esf", piece, up_weight, preferred_element_type=jnp.float32)
    hidden = (jax.nn.silu(gate) * upper).astype(jnp.bfloat16)
    return jnp.einsum(
        "esf,efd->esd", hidden, down_weight, preferred_element_type=jnp.float32
    ).astype(jnp.bfloat16)


def unit_lower_inverse(system):
    size = system.shape[-1]
    if size == 1:
        return jnp.ones_like(system)
    half = size // 2
    both = unit_lower_inverse(jnp.stack([system[..., :half, :half], system[..., half:, half:]]))
    first, second = (both[0], both[1])
    corner = -jnp.einsum(
        "...ij,...jk->...ik",
        second,
        jnp.einsum(
            "...ij,...jk->...ik", system[..., half:, :half], first, precision=lax.Precision.HIGHEST
        ),
        precision=lax.Precision.HIGHEST,
    )
    top = jnp.concatenate([first, jnp.zeros_like(first)], axis=-1)
    bottom = jnp.concatenate([corner, second], axis=-1)
    return jnp.concatenate([top, bottom], axis=-2)


def join_maps(earlier, later):
    first_map, first_state = earlier
    next_map, next_state = later
    joined_map = jnp.einsum("hij,hjk->hik", next_map, first_map, precision=lax.Precision.HIGHEST)
    joined_state = (
        jnp.einsum("hij,hjv->hiv", next_map, first_state, precision=lax.Precision.HIGHEST)
        + next_state
    )
    return (joined_map, joined_state)


def per_device(
    tokens_in,
    expert_ids,
    route_weight,
    first_gain,
    gate_weight,
    up_weight,
    down_weight,
    second_gain,
    mixer_weight,
    gating_weight,
    filter_taps,
    decay_log,
    decay_bias,
    output_gain,
):
    n_outer = lax.axis_size("outer")
    n_inner = lax.axis_size("inner")
    n_dev = n_outer * n_inner
    tok_count, width = tokens_in.shape
    top_count = expert_ids.shape[1]
    local_experts = gate_weight.shape[0]
    experts_all = local_experts * n_dev
    capacity = max(2, 6 * tok_count * top_count // (5 * experts_all))
    normed_first = rms_scale(tokens_in, first_gain).astype(jnp.bfloat16)
    mix_weight = route_weight / jnp.sum(route_weight, axis=1, keepdims=True)
    flat_ids = expert_ids
    target = flat_ids % local_experts * (n_dev * capacity) + flat_ids // local_experts * capacity
    onehot = (
        flat_ids[:, :, None] == jnp.arange(experts_all, dtype=jnp.int32)[None, None, :]
    ).astype(jnp.int32)
    counted = jnp.sum(onehot, axis=1)
    before = jnp.cumsum(counted, axis=0) - counted
    slot_index = jnp.sum(before[:, None, :] * onehot, axis=2)
    target = target + slot_index
    slots = jnp.arange(n_dev * local_experts * capacity, dtype=jnp.int32)
    hits = target[:, :, None] == slots[None, None, :]
    dispatch = jnp.any(hits, axis=1).astype(jnp.bfloat16)
    outgoing = jnp.einsum(
        "ts,td->sd", dispatch, normed_first, preferred_element_type=jnp.float32
    ).astype(jnp.bfloat16)
    outgoing = outgoing.reshape(local_experts, n_dev * capacity, width)
    served = run_experts(
        lax.all_to_all(outgoing, ("outer", "inner"), split_axis=1, concat_axis=1, tiled=True),
        gate_weight,
        up_weight,
        down_weight,
    )
    returned = lax.all_to_all(served, ("outer", "inner"), split_axis=1, concat_axis=1, tiled=True)
    returned = returned.reshape(-1, width)
    combine = jnp.sum(jnp.where(hits, mix_weight[:, :, None], 0.0), axis=1)
    combine_hi = combine.astype(jnp.bfloat16)
    combine_lo = (combine - combine_hi.astype(jnp.float32)).astype(jnp.bfloat16)
    mixture = jnp.dot(combine_hi, returned, preferred_element_type=jnp.float32) + jnp.dot(
        combine_lo, returned, preferred_element_type=jnp.float32
    )
    hidden_out = (tokens_in.astype(jnp.float32) + mixture).astype(jnp.bfloat16)
    normed_second = rms_scale(hidden_out, second_gain).astype(jnp.bfloat16)
    mixed = jnp.dot(
        normed_second,
        lax.all_gather(mixer_weight, "inner", axis=1, tiled=True),
        preferred_element_type=jnp.float32,
    )
    projected = mixed.astype(jnp.bfloat16)
    gating = jnp.dot(normed_second, gating_weight, preferred_element_type=jnp.float32)
    taps = filter_taps.shape[0]
    rim = shifted(projected[tok_count - (taps - 1) :], ("outer", "inner"), 1)
    padded = jnp.concatenate([rim, projected], axis=0).astype(jnp.float32)
    filtered = jnp.zeros(projected.shape, jnp.float32)
    for tap_index in range(taps):
        filtered = (
            filtered
            + filter_taps[tap_index].astype(jnp.float32) * padded[tap_index : tap_index + tok_count]
        )
    filtered = jax.nn.silu(filtered)
    head_dim = output_gain.shape[0]
    value_heads = decay_log.shape[0]
    key_heads = (projected.shape[1] - value_heads * head_dim) // (2 * head_dim)
    ratio = value_heads // key_heads
    queries = unit_heads(
        filtered[:, : key_heads * head_dim].reshape(tok_count, key_heads, head_dim)
    ) * head_dim ** (-0.5)
    keys = unit_heads(
        filtered[:, key_heads * head_dim : 2 * key_heads * head_dim].reshape(
            tok_count, key_heads, head_dim
        )
    )
    values = filtered[:, 2 * key_heads * head_dim :].reshape(tok_count, value_heads, head_dim)
    queries = jnp.repeat(queries, ratio, axis=1)
    keys = jnp.repeat(keys, ratio, axis=1)
    strength = jax.nn.sigmoid(gating[:, :value_heads]).T
    log_decay = (-jnp.exp(decay_log) * jax.nn.softplus(gating[:, value_heads:] + decay_bias)).T
    cumulative = jnp.cumsum(log_decay, axis=1)
    positions = jnp.arange(tok_count)
    lower_incl = positions[:, None] >= positions[None, :]
    lower_strict = positions[:, None] > positions[None, :]
    spread = cumulative[:, :, None] - cumulative[:, None, :]
    decay_mat = jnp.where(lower_incl, jnp.exp(jnp.where(lower_incl, spread, 0.0)), 0.0)
    key_major = keys.transpose(1, 0, 2)
    query_leading = queries.transpose(1, 0, 2)
    value_major = values.transpose(1, 0, 2)
    key_inner = jnp.einsum("htd,hid->hti", key_major, key_major, precision=lax.Precision.HIGHEST)
    lower_part = jnp.where(lower_strict, decay_mat * key_inner, 0.0) * strength[:, :, None]
    system = lower_part + jnp.eye(tok_count, dtype=jnp.float32)
    growth = jnp.exp(cumulative)
    scaled_keys = key_major * (strength * growth)[:, :, None]
    scaled_values = value_major * strength[:, :, None]
    inverse = unit_lower_inverse(system)
    key_resolved = jnp.einsum("hts,hsd->htd", inverse, scaled_keys, precision=lax.Precision.HIGHEST)
    value_resolved = jnp.einsum(
        "hts,hsd->htd", inverse, scaled_values, precision=lax.Precision.HIGHEST
    )
    tail = jnp.exp(cumulative[:, -1:] - cumulative)
    trailing_keys = key_major * tail[:, :, None]
    eye_heads = jnp.broadcast_to(
        jnp.eye(head_dim, dtype=jnp.float32), (value_heads, head_dim, head_dim)
    )
    state_map = growth[:, -1][:, None, None] * eye_heads - jnp.einsum(
        "htk,htj->hkj", trailing_keys, key_resolved, precision=lax.Precision.HIGHEST
    )
    state_increment = jnp.einsum(
        "xbe,xbz->xez", trailing_keys, value_resolved, precision=lax.Precision.HIGHEST
    )
    identity = (eye_heads, jnp.zeros_like(state_increment))
    inner_pre = prefix_2((state_map, state_increment), "inner", join_maps, identity)
    inclusive = join_maps(inner_pre, (state_map, state_increment))
    group = spread_2(shortened(jnp.stack(inclusive)), "inner", n_inner - 1)
    outer_pre = entering((group[0], group[1]), "outer", join_maps, identity)
    prefix = join_maps(outer_pre, inner_pre)
    initial_state = prefix[1]
    updates = value_resolved - jnp.einsum(
        "mwx,mxd->mwd", key_resolved, initial_state, precision=lax.Precision.HIGHEST
    )
    query_key = (
        jnp.einsum("htd,hid->hti", query_leading, key_major, precision=lax.Precision.HIGHEST)
        * decay_mat
    )
    carried = (
        jnp.einsum("mwx,mxd->mwd", query_leading, initial_state, precision=lax.Precision.HIGHEST)
        * growth[:, :, None]
    )
    attended = carried + jnp.einsum(
        "hti,hiv->htv", query_key, updates, precision=lax.Precision.HIGHEST
    )
    attended = attended.transpose(1, 0, 2)
    core_out = (
        rms_scale(attended, output_gain)
        .astype(jnp.bfloat16)
        .reshape(tok_count, value_heads * head_dim)
    )
    return (hidden_out, core_out)


def solution(mesh):
    return jax.shard_map(
        per_device,
        mesh=mesh,
        in_specs=(
            P(("outer", "inner"), None),
            P(("outer", "inner"), None),
            P(("outer", "inner"), None),
            P(),
            P(("outer", "inner"), None, None),
            P(("outer", "inner"), None, None),
            P(("outer", "inner"), None, None),
            P(),
            P(None, "inner"),
            P(),
            P(),
            P(),
            P(),
            P(),
        ),
        out_specs=(P(("outer", "inner"), None), P(("outer", "inner"), None)),
        check_vma=False,
    )
```

profile of v0, /device:TPU:1, one launch (start us, length us, event | category | flops | bytes accessed | tf_op | source)
XLA Modules:
  0.0 724.9 jit_solution(11721711058515278131)
XLA Ops:
  7.9 0.9 convert_reduce_fusion
  9.1 1.2 fusion.41
  10.3 1.1 select_reduce_fusion.1
  12.2 1.3 fusion.15
  13.5 2.9 convolution_convert_fusion
  16.4 13.0 %copy.112 = bf16[2,768,2048]{2,0,1:T(2,128)(2,1)S(1)} copy(bf16[2,768,2048]{2,1,0:T(8,128)(2,1)S(1)} %bitcast.186) | data formatting | bytes 12582912 | tf_op jit(solution)/shard_map/reshape | solution.py:157
  29.5 98.2 %all_to_all.10 = bf16[2,768,2048]{2,0,1:T(2,128)(2,1)S(1)} all-to-all(bf16[2,768,2048]{2,0,1:T(2,128)(2,1)S(1)} %copy.112), channel_id=1, replica_groups=mesh['outer'=8,'inner'=16] {'outer','inner'}, dimensions={1} | all-to-all | bytes 12582912 | tf_op jit(solution)/shard_map/all_to_all | solution.py:159
  127.6 2.7 copy-done.12
  130.3 5.3 fusion.18
  135.6 16.5 %convolution_convert_fusion.2 = bf16[2,768,2048]{2,1,0:T(8,128)(2,1)} fusion(bf16[2,512,2048]{2,1,0:T(8,128)(2,1)} %param.24, f32[2,768,512]{2,1,0:T(8,128)} %fusion.18, bf16[2,2048,512]{2,1,0:T(8,128)(2,1)} %param.23, bf16[2,768,2048]{2,0,1:T(2,128)(2,1)} %copy-done.12), kind=kOutput, calls=%fused_computation.26 | convolution fusion | flops 6450315264 | bytes 24117248 | tf_op jit(solution)/shard_map/esf,efd->esd/dot_general | solution.py:80
  152.1 12.7 %copy.115 = bf16[2,768,2048]{2,0,1:T(2,128)(2,1)} copy(bf16[2,768,2048]{2,1,0:T(8,128)(2,1)} %convolution_convert_fusion.2) | data formatting | bytes 12582912 | tf_op jit(solution)/shard_map/convert_element_type | solution.py:82
  164.8 12.8 %all-to-all-start.1 = ((bf16[2,768,2048]{2,0,1:T(2,128)(2,1)}), bf16[2,768,2048]{2,0,1:T(2,128)(2,1)}, u32[]{:S(2)}, u32[]{:S(2)}) async-start(bf16[2,768,2048]{2,0,1:T(2,128)(2,1)} %copy.115), calls=%async_computation.1 | async-start | bytes 12582912 | tf_op jit(solution)/shard_map/all_to_all | solution.py:164
  178.0 1.2 select_reduce_fusion
  179.3 83.1 %all-to-all-done.1 = bf16[2,768,2048]{2,0,1:T(2,128)(2,1)} async-done(((bf16[2,768,2048]{2,0,1:T(2,128)(2,1)}), bf16[2,768,2048]{2,0,1:T(2,128)(2,1)}, u32[]{:S(2)}, u32[]{:S(2)}) %all-to-all-start.1) | async-done | bytes 6291488 | tf_op jit(solution)/shard_map/all_to_all | solution.py:164
  262.3 5.7 copy.116
  268.0 1.0 fusion.80
  269.1 1.4 fusion.38
  271.5 8.2 %convolution_convert_fusion.1 = bf16[128,4096]{1,0:T(8,128)(2,1)S(1)} fusion(bf16[2048,4096]{1,0:T(8,128)(2,1)} %all-gather.8.cloned.1.call-done, bf16[128,2048]{1,0:T(8,128)(2,1)S(1)} %get-tuple-element.227, f32[2048]{0:T(1024)S(1)} %copy-done.36, f32[128]{0:T(128)S(1)} %add_rsqrt_fusion.3), kind=kOutput, calls=%fused_computation.25 | convolution fusion | flops 2149056512 | bytes 18358784 | tf_op jit(solution)/shard_map/dot_general | solution.py:174
  279.7 9.9 %collective-permute-start = (bf16[3,4096]{1,0:T(4,128)(2,1)S(1)}, bf16[3,4096]{1,0:T(4,128)(2,1)S(1)}, u32[]{:S(2)}, u32[]{:S(2)}) collective-permute-start(bf16[3,4096]{1,0:T(4,128)(2,1)S(1)} %slice.199), channel_id=1, source_target_pairs={{0,1},{1,2},{2,3},{3,4},{4,5},{5,6},{6,7},{7,8},{8,9},{9,10},{10,1... | collective-permute-start | bytes 73736 | tf_op jit(solution)/shard_map/ppermute | solution.py:10
  290.6 1.2 divide_multiply_fusion
  291.9 1.0 slice_bitcast_fusion.13
  293.7 2.4 fusion.34
  297.9 1.4 fusion.52
  299.3 1.5 copy.119
  300.8 1.5 copy.120
  303.4 1.3 copy.134
  304.7 1.2 copy.123
  305.9 1.2 copy.135
  307.1 4.7 fusion.111
  311.9 4.8 convolution_negate_fusion.5
  316.7 0.9 select_maximum_fusion.5
  317.7 3.1 fusion.73
  320.9 1.8 convolution_negate_fusion.4
  323.2 1.0 fusion.71
  324.2 1.0 convolution_negate_fusion.3
  330.4 1.6 bitcast_multiply_fusion
  332.0 1.3 fusion.45
  333.3 3.0 fusion.119
  336.6 2.8 fusion.78
  339.3 2.8 fusion.118
  342.3 66.4 %all-gather.16.cloned.1.call-done = bf16[256,128,128]{2,1,0:T(8,128)(2,1)} async-done(((bf16[16,128,128]{2,1,0:T(8,128)(2,1)}), bf16[256,128,128]{2,1,0:T(8,128)(2,1)}) %all-gather.16.cloned.1.call-update) | async-done | bytes 8388624 | tf_op jit(solution)/shard_map/all_gather | solution.py:16
  408.6 72.5 %all-gather.14.cloned.1.call-done = bf16[256,128,128]{2,1,0:T(8,128)(2,1)} async-done(((bf16[16,128,128]{2,1,0:T(8,128)(2,1)}), bf16[256,128,128]{2,1,0:T(8,128)(2,1)}) %all-gather.14.cloned.1.call-update) | async-done | bytes 8388624 | tf_op jit(solution)/shard_map/all_gather | solution.py:16
  481.6 1.2 fusion.36
  482.8 2.4 fusion.37
  485.2 1.1 maximum_select_fusion
  486.4 141.0 %all-reduce.9.cloned.1.call-done = bf16[2,16,128,128]{3,2,1,0:T(8,128)(2,1)} async-done(((bf16[2,16,128,128]{3,2,1,0:T(8,128)(2,1)}), bf16[2,16,128,128]{3,2,1,0:T(8,128)(2,1)}) %all-reduce.9.cloned.1.call-update) | async-done | bytes 1048592 | tf_op jit(solution)/shard_map/psum | solution.py:43
  627.4 2.3 fusion.116
  631.1 1.0 copy-done.4
  632.0 3.3 convolution_multiply_fusion
  635.3 28.0 %all-gather.10.cloned.1.call-done = bf16[8,16,128,128]{3,2,1,0:T(8,128)(2,1)} async-done(((bf16[1,16,128,128]{3,2,1,0:T(8,128)(2,1)}), bf16[8,16,128,128]{3,2,1,0:T(8,128)(2,1)}) %all-gather.10.cloned.1.call-update) | async-done | bytes 4194320 | tf_op jit(solution)/shard_map/all_gather | solution.py:49
  663.3 33.7 %all-gather.12.cloned.1.call-done = bf16[8,16,128,128]{3,2,1,0:T(8,128)(2,1)} async-done(((bf16[1,16,128,128]{3,2,1,0:T(8,128)(2,1)}), bf16[8,16,128,128]{3,2,1,0:T(8,128)(2,1)}) %all-gather.12.cloned.1.call-update) | async-done | bytes 4194320 | tf_op jit(solution)/shard_map/all_gather | solution.py:49
  697.1 12.6 %while.27 = (s32[]{:T(128)}, bf16[16,128,128]{2,1,0:T(8,128)(2,1)S(1)}, s32[]{:T(128)}, bf16[8,16,128,128]{3,2,1,0:T(8,128)(2,1)}, bf16[8,16,128,128]{3,2,1,0:T(8,128)(2,1)}, /*index=5*/s32[]{:T(128)}, s32[]{:T(128)}) while((s32[]{:T(128)}, bf16[16,128,128]{2,1,0:T(8,128)(2,1)S(1)}, s32[]{:T(128)}, ...), condition=%wide.region_15.16_spmd.clone, body=%wide.region_14.15_spmd.clone.sunk | while | flops 68157440 | bytes 3672671 | solution.py:64
  697.1 1.5 fusion.173
  698.7 1.5 fusion.173
  700.3 1.5 fusion.173
  701.9 1.5 fusion.173
  703.4 1.5 fusion.173
  705.0 1.5 fusion.173
  706.6 1.5 fusion.173
  708.2 1.5 fusion.173
  711.2 1.2 convolution_subtract_fusion
  712.5 1.9 fusion.31
  714.4 1.9 multiply_reduce_fusion
  716.6 1.0 copy.129
  (173 shorter events, 17.4 us)
Async XLA Ops:
  7.2 263.3 %copy-start = (bf16[2048,32]{0,1:T(8,128)(2,1)S(1)}, bf16[2048,32]{0,1:T(8,128)(2,1)}, u32[]{:S(2)}) copy-start(bf16[2048,32]{0,1:T(8,128)(2,1)} %param.27) | copy-start | bytes 393220
  7.2 264.3 %all-gather.8.cloned.1.call-start = ((), (), s32[]{:S(2)}) async-start(), calls=%async_computation.2 | async-start | bytes 17825792 | tf_op jit(solution)/shard_map/all_gather | solution.py:176
  29.4 100.8 %copy-start.44 = (bf16[2,2048,512]{2,1,0:T(8,128)(2,1)S(1)}, bf16[2,2048,512]{2,1,0:T(8,128)(2,1)}, u32[]{:S(2)}) copy-start(bf16[2,2048,512]{2,1,0:T(8,128)(2,1)} %param.22) | copy-start | bytes 12582916
  127.6 2.7 copy-start.12
  164.8 13.1 %copy-start.41 = (f32[128,10]{0,1:T(8,128)S(1)}, f32[128,10]{0,1:T(8,128)}, u32[]{:S(2)}) copy-start(f32[128,10]{0,1:T(8,128)} %param.20) | copy-start | bytes 15364
  164.8 13.2 %copy-start.45 = (f32[16]{0:T(128)S(1)}, f32[16]{0:T(128)}, u32[]{:S(2)}) copy-start(f32[16]{0:T(128)} %param.29) | copy-start | bytes 196
  164.8 14.4 %copy-start.35 = (bf16[4,4096]{1,0:T(4,128)(2,1)S(1)}, bf16[4,4096]{1,0:T(4,128)(2,1)}, u32[]{:S(2)}) copy-start(bf16[4,4096]{1,0:T(4,128)(2,1)} %param.28) | copy-start | bytes 98308
  164.8 97.5 %all-to-all-start.1 = ((bf16[2,768,2048]{2,0,1:T(2,128)(2,1)}), bf16[2,768,2048]{2,0,1:T(2,128)(2,1)}, u32[]{:S(2)}, u32[]{:S(2)}) async-start(bf16[2,768,2048]{2,0,1:T(2,128)(2,1)} %copy.115), calls=%async_computation.1 | async-start | bytes 12582912 | tf_op jit(solution)/shard_map/all_to_all | solution.py:164
  177.6 231.0 %all-gather.16.cloned.1.call-start = ((), (), s32[]{:S(2)}) async-start(), calls=%async_computation.7 | async-start | bytes 8912896 | tf_op jit(solution)/shard_map/all_gather | solution.py:16
  178.0 115.7 %copy-start.33 = (pred[128,128]{1,0:T(8,128)(4,1)}, pred[128,128]{1,0:T(8,128)(4,1)S(1)}, u32[]{:S(2)}) copy-start(pred[128,128]{1,0:T(8,128)(4,1)S(1)} %get-tuple-element.234) | copy-start | bytes 49156
  268.0 1.0 copy-start.13
  269.1 1.4 copy-start.36
  269.1 1.8 copy-start.42
  270.5 9.2 %copy-start.29 = (bf16[128,2048]{1,0:T(8,128)(2,1)}, bf16[128,2048]{1,0:T(8,128)(2,1)S(1)}, u32[]{:S(2)}) copy-start(bf16[128,2048]{1,0:T(8,128)(2,1)S(1)} %get-tuple-element.227) | copy-start | bytes 1572868
  279.7 10.6 %collective-permute-start = (bf16[3,4096]{1,0:T(4,128)(2,1)S(1)}, bf16[3,4096]{1,0:T(4,128)(2,1)S(1)}, u32[]{:S(2)}, u32[]{:S(2)}) collective-permute-start(bf16[3,4096]{1,0:T(4,128)(2,1)S(1)} %slice.199), channel_id=1, source_target_pairs={{0,1},{1,2},{2,3},{3,4},{4,5},{5,6},{6,7},{7,8},{8,9},{9,10},{10,1... | collective-permute-start | bytes 73736 | tf_op jit(solution)/shard_map/ppermute | solution.py:10
  291.9 1.6 copy-start.10
  293.7 3.1 copy-start.2
  296.3 0.8 copy-start.16
  296.6 0.8 copy-start.18
  296.6 1.0 copy-start.20
  296.8 0.9 copy-start.22
  296.8 1.1 copy-start.24
  297.6 19.1 %copy-start.26 = (f32[1,2,2,2,16,8,8]{6,5,4,3,2,1,0:T(8,128)}, f32[1,2,2,2,16,8,8]{6,5,4,3,2,1,0:T(8,128)S(1)}, u32[]{:S(2)}) copy-start(f32[1,2,2,2,16,8,8]{6,5,4,3,2,1,0:T(8,128)S(1)} %get-tuple-element.201) | copy-start | bytes 98308
  297.6 19.1 %copy-start.27 = (f32[1,2,2,2,16,8,8]{6,5,4,3,2,1,0:T(8,128)}, f32[1,2,2,2,16,8,8]{6,5,4,3,2,1,0:T(8,128)S(1)}, u32[]{:S(2)}) copy-start(f32[1,2,2,2,16,8,8]{6,5,4,3,2,1,0:T(8,128)S(1)} %get-tuple-element.202) | copy-start | bytes 98308
  307.1 9.5 %copy-start.30 = (f32[1,2,2,2,2,2,16,2,2]{8,7,6,5,4,3,2,1,0:T(2,128)S(1)}, f32[1,2,2,2,2,2,16,2,2]{8,7,6,5,4,3,2,1,0:T(2,128)}, u32[]{:S(2)}) copy-start(f32[1,2,2,2,2,2,16,2,2]{8,7,6,5,4,3,2,1,0:T(2,128)} %copy.134) | copy-start | bytes 24580
  307.1 9.5 %copy-start.31 = (f32[1,2,2,2,2,2,16,2,2]{8,7,6,5,4,3,2,1,0:T(2,128)S(1)}, f32[1,2,2,2,2,2,16,2,2]{8,7,6,5,4,3,2,1,0:T(2,128)}, u32[]{:S(2)}) copy-start(f32[1,2,2,2,2,2,16,2,2]{8,7,6,5,4,3,2,1,0:T(2,128)} %copy.135) | copy-start | bytes 24580
  317.6 5.5 copy-start.23
  317.7 5.5 copy-start.25
  323.1 2.3 copy-start.19
  323.2 2.3 copy-start.21
  325.4 1.6 copy-start.17
  328.7 1.7 copy-start.38
  328.7 1.7 copy-start.39
  329.0 3.0 copy-start.11
  329.7 6.6 copy-start.14
  329.7 6.6 copy-start.15
  332.0 4.4 copy-start.40
  333.3 8.9 %copy-start.6 = (f32[16,128,128]{2,1,0:T(8,128)}, f32[16,128,128]{2,1,0:T(8,128)S(1)}, u32[]{:S(2)}) copy-start(f32[16,128,128]{2,1,0:T(8,128)S(1)} %fusion.45) | copy-start | bytes 3145732
  336.3 144.8 %all-gather.14.cloned.1.call-start = ((), (), s32[]{:S(2)}) async-start(), calls=%async_computation.6 | async-start | bytes 8912896 | tf_op jit(solution)/shard_map/all_gather | solution.py:16
  339.3 2.8 copy-start.8
  342.2 285.2 %all-reduce.9.cloned.1.call-start = ((), (), s32[]{:S(2)}) async-start(), calls=%async_computation.3 | async-start | bytes 2097152 | tf_op jit(solution)/shard_map/psum | solution.py:43
  485.2 145.1 %copy-start.32 = (f32[16,8,8,128]{3,1,2,0:T(8,128)S(1)}, f32[16,8,8,128]{3,1,2,0:T(8,128)}, u32[]{:S(2)}) copy-start(f32[16,8,8,128]{3,1,2,0:T(8,128)} %get-tuple-element.186) | copy-start | bytes 1572868
  486.3 145.7 %copy-start.34 = (pred[128,128]{1,0:T(8,128)(4,1)S(1)}, pred[128,128]{1,0:T(8,128)(4,1)}, u32[]{:S(2)}) copy-start(pred[128,128]{1,0:T(8,128)(4,1)} %copy-done.33) | copy-start | bytes 49156
  486.3 177.0 %all-gather.10.cloned.1.call-start = ((), (), s32[]{:S(2)}) async-start(), calls=%async_computation.4 | async-start | bytes 4718592 | tf_op jit(solution)/shard_map/all_gather | solution.py:49
  629.7 67.4 %all-gather.12.cloned.1.call-start = ((), (), s32[]{:S(2)}) async-start(), calls=%async_computation.5 | async-start | bytes 4718592 | tf_op jit(solution)/shard_map/all_gather | solution.py:49
  630.3 1.8 copy-start.3
  631.1 1.0 copy-start.4
  709.7 1.2 copy-start.7
  709.7 1.5 copy-start.9
  709.7 2.7 copy-start.5
  709.7 2.7 copy-start.37
  711.2 3.1 copy-start.28
  712.4 3.9 copy-start.43
  712.5 5.1 copy-start.1
Sparse Core Ops, SparseCore 0:
  10.1 225.6 all-gather.7
  336.4 72.1 all-gather.15
  410.8 70.3 all-gather.13
  486.4 140.9 all-reduce.8
  629.8 33.4 all-gather.9
  664.9 32.1 all-gather.11
where the time goes:
time: 731 us; the launch traced here: 725 us
  waiting for transfers between devices  426 us (58%)
  blocking collectives  98.2 us (13%)
  matrix products  93.1 us (13%)
  local copies, waits for them, and re-layouts  50 us (7%)
  starting transfers between devices  23.2 us (3%)
  other arithmetic  18.3 us (3%)
  between operations  15.7 us (2%)
    psum x1, waiting for transfers between devices, spread_2(): return lax.psum(kept, axis)  141 us
    all_gather x2, waiting for transfers between devices, prefix_2(): lax.all_gather(a.astype(kind), axis)  139 us
    all_to_all x1, blocking collectives, per_device(): lax.all_to_all(outgoing, ('outer', 'inner'), split_axis=1, concat_axis=1,...  98.2 us
    all_to_all x1, waiting for transfers between devices, per_device(): lax.all_to_all(served, ('outer', 'inner'), split_axis=1, concat_axis=1, t...  83.1 us
    all_gather x2, waiting for transfers between devices, entering(): lax.all_gather(part.astype(kind), axis)  61.7 us
    dot_general x1, matrix products, run_experts(): jnp.einsum('esf,efd->esd', hidden, down_weight, preferred_element_type=jn...  16.5 us
    dot_general x10, matrix products, join_maps(): jnp.einsum('hij,hjv->hiv', next_map, first_state, precision=lax.Precision...  15.1 us
  transfers between devices with their start and end apart: 8, of which 6 were waited for; matrix products, arithmetic and copies ran while one was open for 11% of the time, Pallas kernels for 0%

commit v1 on v0

--- a/solution.py
+++ b/solution.py
@@ -40,7 +40,7 @@
 
 def spread_2(value, axis, source):
     kept = jnp.where(lax.axis_index(axis) == source, value, 0).astype(value.dtype)
-    return lax.psum(kept, axis)
+    return jnp.sum(lax.all_gather(kept, axis), axis=0)
 
 
 def entering(x, axis, combine, identity):

time: 731 us -> 763 us (1.044)
  waiting for transfers between devices: 426 us -> 449 us
  other arithmetic: 18.3 us -> 27.5 us
    all_gather x0 -> x1, waiting for transfers between devices: none -> 167 us  [spread_2(): return jnp.sum(lax.all_gather(kept, axis), axis=0)]
    psum x1 -> x0, waiting for transfers between devices: 141 us -> none  [spread_2(): return lax.psum(kept, axis)]
    reduce_sum x0 -> x1, other arithmetic: none -> 9.28 us  [spread_2(): return jnp.sum(lax.all_gather(kept, axis), axis=0)]
  transfers between devices with their start and end apart: 8 -> 8, of which waited for: 6 -> 6; matrix products, arithmetic and copies ran while one was open for 11% -> 10% of each run, Pallas kernels for 0% -> 0%
where the time goes in v1:
time: 763 us; the launch traced here: 757 us
  waiting for transfers between devices  449 us (59%)
  blocking collectives  98.2 us (13%)
  matrix products  93.1 us (12%)
  local copies, waits for them, and re-layouts  49.9 us (7%)
  other arithmetic  27.5 us (4%)
  starting transfers between devices  23.4 us (3%)
  between operations  15.7 us (2%)
    all_gather x1, waiting for transfers between devices, spread_2(): return jnp.sum(lax.all_gather(kept, axis), axis=0)  167 us
    all_gather x2, waiting for transfers between devices, prefix_2(): lax.all_gather(a.astype(kind), axis)  138 us
    all_to_all x1, blocking collectives, per_device(): lax.all_to_all(outgoing, ('outer', 'inner'), split_axis=1, concat_axis=1,...  98.2 us
    all_to_all x1, waiting for transfers between devices, per_device(): lax.all_to_all(served, ('outer', 'inner'), split_axis=1, concat_axis=1, t...  83 us
    all_gather x2, waiting for transfers between devices, entering(): lax.all_gather(part.astype(kind), axis)  59.6 us
    dot_general x1, matrix products, run_experts(): jnp.einsum('esf,efd->esd', hidden, down_weight, preferred_element_type=jn...  16.6 us
  transfers between devices with their start and end apart: 8, of which 6 were waited for; matrix products, arithmetic and copies ran while one was open for 10% of the time, Pallas kernels for 0%

profile of v1, /device:TPU:1, one launch (start us, length us, event | category | flops | bytes accessed | tf_op | source)
XLA Modules:
  0.0 757.2 jit_solution(7710131618361502874)
XLA Ops:
  9.1 1.2 fusion.41
  10.3 1.1 select_reduce_fusion.1
  12.2 1.3 fusion.15
  13.5 2.9 convolution_convert_fusion
  16.4 13.0 %copy.112 = bf16[2,768,2048]{2,0,1:T(2,128)(2,1)S(1)} copy(bf16[2,768,2048]{2,1,0:T(8,128)(2,1)S(1)} %bitcast.186) | data formatting | bytes 12582912 | tf_op jit(solution)/shard_map/reshape | solution.py:157
  29.5 98.2 %all_to_all.10 = bf16[2,768,2048]{2,0,1:T(2,128)(2,1)S(1)} all-to-all(bf16[2,768,2048]{2,0,1:T(2,128)(2,1)S(1)} %copy.112), channel_id=1, replica_groups=mesh['outer'=8,'inner'=16] {'outer','inner'}, dimensions={1} | all-to-all | bytes 12582912 | tf_op jit(solution)/shard_map/all_to_all | solution.py:159
  127.6 2.7 copy-done.12
  130.3 5.3 fusion.18
  135.6 16.6 %convolution_convert_fusion.2 = bf16[2,768,2048]{2,1,0:T(8,128)(2,1)} fusion(bf16[2,512,2048]{2,1,0:T(8,128)(2,1)} %param.24, f32[2,768,512]{2,1,0:T(8,128)} %fusion.18, bf16[2,2048,512]{2,1,0:T(8,128)(2,1)} %param.23, bf16[2,768,2048]{2,0,1:T(2,128)(2,1)} %copy-done.12), kind=kOutput, calls=%fused_computation.26 | convolution fusion | flops 6450315264 | bytes 24117248 | tf_op jit(solution)/shard_map/esf,efd->esd/dot_general | solution.py:80
  152.2 12.7 %copy.115 = bf16[2,768,2048]{2,0,1:T(2,128)(2,1)} copy(bf16[2,768,2048]{2,1,0:T(8,128)(2,1)} %convolution_convert_fusion.2) | data formatting | bytes 12582912 | tf_op jit(solution)/shard_map/convert_element_type | solution.py:82
  164.8 12.8 %all-to-all-start.1 = ((bf16[2,768,2048]{2,0,1:T(2,128)(2,1)}), bf16[2,768,2048]{2,0,1:T(2,128)(2,1)}, u32[]{:S(2)}, u32[]{:S(2)}) async-start(bf16[2,768,2048]{2,0,1:T(2,128)(2,1)} %copy.115), calls=%async_computation.1 | async-start | bytes 12582912 | tf_op jit(solution)/shard_map/all_to_all | solution.py:164
  178.1 1.2 select_reduce_fusion
  179.3 83.0 %all-to-all-done.1 = bf16[2,768,2048]{2,0,1:T(2,128)(2,1)} async-done(((bf16[2,768,2048]{2,0,1:T(2,128)(2,1)}), bf16[2,768,2048]{2,0,1:T(2,128)(2,1)}, u32[]{:S(2)}, u32[]{:S(2)}) %all-to-all-start.1) | async-done | bytes 6291488 | tf_op jit(solution)/shard_map/all_to_all | solution.py:164
  262.3 5.7 copy.116
  268.0 1.0 fusion.80
  269.1 1.4 fusion.38
  271.4 8.2 %convolution_convert_fusion.1 = bf16[128,4096]{1,0:T(8,128)(2,1)S(1)} fusion(bf16[2048,4096]{1,0:T(8,128)(2,1)} %all-gather.9.cloned.1.call-done, bf16[128,2048]{1,0:T(8,128)(2,1)S(1)} %get-tuple-element.227, f32[2048]{0:T(1024)S(1)} %copy-done.35, f32[128]{0:T(128)S(1)} %add_rsqrt_fusion.3), kind=kOutput, calls=%fused_computation.25 | convolution fusion | flops 2149056512 | bytes 18358784 | tf_op jit(solution)/shard_map/dot_general | solution.py:174
  279.7 10.1 %collective-permute-start = (bf16[3,4096]{1,0:T(4,128)(2,1)S(1)}, bf16[3,4096]{1,0:T(4,128)(2,1)S(1)}, u32[]{:S(2)}, u32[]{:S(2)}) collective-permute-start(bf16[3,4096]{1,0:T(4,128)(2,1)S(1)} %slice.199), channel_id=1, source_target_pairs={{0,1},{1,2},{2,3},{3,4},{4,5},{5,6},{6,7},{7,8},{8,9},{9,10},{10,1... | collective-permute-start | bytes 73736 | tf_op jit(solution)/shard_map/ppermute | solution.py:10
  290.8 1.2 divide_multiply_fusion
  292.1 1.0 slice_bitcast_fusion.13
  293.9 2.4 fusion.34
  298.1 1.4 fusion.52
  299.5 1.5 copy.119
  301.0 1.5 copy.120
  303.6 1.2 copy.134
  304.8 1.2 copy.123
  306.1 1.2 copy.135
  307.3 4.7 fusion.111
  312.1 4.8 convolution_negate_fusion.5
  317.8 3.1 fusion.73
  321.0 1.8 convolution_negate_fusion.4
  323.3 1.0 fusion.71
  324.4 1.0 convolution_negate_fusion.3
  330.6 1.6 bitcast_multiply_fusion
  332.1 1.3 fusion.45
  333.4 3.0 fusion.119
  336.7 2.8 fusion.78
  339.5 2.8 fusion.118
  342.4 65.7 %all-gather.19.cloned.1.call-done = bf16[256,128,128]{2,1,0:T(8,128)(2,1)} async-done(((bf16[16,128,128]{2,1,0:T(8,128)(2,1)}), bf16[256,128,128]{2,1,0:T(8,128)(2,1)}) %all-gather.19.cloned.1.call-update) | async-done | bytes 8388624 | tf_op jit(solution)/shard_map/all_gather | solution.py:16
  408.1 72.5 %all-gather.17.cloned.1.call-done = bf16[256,128,128]{2,1,0:T(8,128)(2,1)} async-done(((bf16[16,128,128]{2,1,0:T(8,128)(2,1)}), bf16[256,128,128]{2,1,0:T(8,128)(2,1)}) %all-gather.17.cloned.1.call-update) | async-done | bytes 8388624 | tf_op jit(solution)/shard_map/all_gather | solution.py:16
  481.1 1.1 fusion.36
  482.3 2.4 fusion.37
  484.7 1.1 maximum_select_fusion
  485.9 166.8 %all-gather.11.cloned.1.call-done = bf16[16,2,16,128,128]{4,3,2,1,0:T(8,128)(2,1)} async-done(((bf16[1,2,16,128,128]{4,3,2,1,0:T(8,128)(2,1)}), bf16[16,2,16,128,128]{4,3,2,1,0:T(8,128)(2,1)}) %all-gather.11.cloned.1.call-update) | async-done | bytes 16777232 | tf_op jit(solution)/shard_map/all_gather | solution.py:43
  652.7 9.3 %reduce_sum.101 = bf16[2,16,128,128]{3,2,1,0:T(8,128)(2,1)S(1)} reduce(bf16[16,2,16,128,128]{4,3,2,1,0:T(8,128)(2,1)} %all-gather.11.cloned.1.call-done, bf16[]{:T(256)} %constant.115.clone.1), dimensions={0}, to_apply=%region_13.14 | reduce | flops 7864320 | bytes 17825794 | tf_op jit(solution)/shard_map/reduce_sum | solution.py:43
  662.0 1.0 fusion.116
  663.7 1.2 copy.138
  665.6 1.0 copy-done.4
  666.5 3.3 convolution_multiply_fusion
  669.8 25.9 %all-gather.13.cloned.1.call-done = bf16[8,16,128,128]{3,2,1,0:T(8,128)(2,1)} async-done(((bf16[1,16,128,128]{3,2,1,0:T(8,128)(2,1)}), bf16[8,16,128,128]{3,2,1,0:T(8,128)(2,1)}) %all-gather.13.cloned.1.call-update) | async-done | bytes 4194320 | tf_op jit(solution)/shard_map/all_gather | solution.py:49
  695.7 33.7 %all-gather.15.cloned.1.call-done = bf16[8,16,128,128]{3,2,1,0:T(8,128)(2,1)} async-done(((bf16[1,16,128,128]{3,2,1,0:T(8,128)(2,1)}), bf16[8,16,128,128]{3,2,1,0:T(8,128)(2,1)}) %all-gather.15.cloned.1.call-update) | async-done | bytes 4194320 | tf_op jit(solution)/shard_map/all_gather | solution.py:49
  729.4 12.6 %while.27 = (s32[]{:T(128)}, bf16[16,128,128]{2,1,0:T(8,128)(2,1)S(1)}, s32[]{:T(128)}, bf16[8,16,128,128]{3,2,1,0:T(8,128)(2,1)}, bf16[8,16,128,128]{3,2,1,0:T(8,128)(2,1)}, /*index=5*/s32[]{:T(128)}, s32[]{:T(128)}) while((s32[]{:T(128)}, bf16[16,128,128]{2,1,0:T(8,128)(2,1)S(1)}, s32[]{:T(128)}, ...), condition=%wide.region_15.16_spmd.clone, body=%wide.region_14.15_spmd.clone.sunk | while | flops 68157440 | bytes 3672671 | solution.py:64
  729.5 1.5 fusion.173
  731.1 1.5 fusion.173
  732.7 1.5 fusion.173
  734.2 1.5 fusion.173
  735.8 1.5 fusion.173
  737.4 1.5 fusion.173
  739.0 1.5 fusion.173
  740.6 1.5 fusion.173
  743.6 1.2 convolution_subtract_fusion
  744.9 1.9 fusion.31
  746.8 1.9 multiply_reduce_fusion
  748.9 1.0 copy.129
  (172 shorter events, 19.2 us)
Async XLA Ops:
  7.2 263.3 %copy-start = (bf16[2048,32]{0,1:T(8,128)(2,1)S(1)}, bf16[2048,32]{0,1:T(8,128)(2,1)}, u32[]{:S(2)}) copy-start(bf16[2048,32]{0,1:T(8,128)(2,1)} %param.27) | copy-start | bytes 393220
  7.2 264.3 %all-gather.9.cloned.1.call-start = ((), (), s32[]{:S(2)}) async-start(), calls=%async_computation.2 | async-start | bytes 17825792 | tf_op jit(solution)/shard_map/all_gather | solution.py:176
  29.4 100.8 %copy-start.43 = (bf16[2,2048,512]{2,1,0:T(8,128)(2,1)S(1)}, bf16[2,2048,512]{2,1,0:T(8,128)(2,1)}, u32[]{:S(2)}) copy-start(bf16[2,2048,512]{2,1,0:T(8,128)(2,1)} %param.22) | copy-start | bytes 12582916
  127.6 2.7 copy-start.12
  164.8 13.1 %copy-start.40 = (f32[128,10]{0,1:T(8,128)S(1)}, f32[128,10]{0,1:T(8,128)}, u32[]{:S(2)}) copy-start(f32[128,10]{0,1:T(8,128)} %param.20) | copy-start | bytes 15364
  164.8 13.2 %copy-start.44 = (f32[16]{0:T(128)S(1)}, f32[16]{0:T(128)}, u32[]{:S(2)}) copy-start(f32[16]{0:T(128)} %param.29) | copy-start | bytes 196
  164.8 14.4 %copy-start.34 = (bf16[4,4096]{1,0:T(4,128)(2,1)S(1)}, bf16[4,4096]{1,0:T(4,128)(2,1)}, u32[]{:S(2)}) copy-start(bf16[4,4096]{1,0:T(4,128)(2,1)} %param.28) | copy-start | bytes 98308
  164.8 97.5 %all-to-all-start.1 = ((bf16[2,768,2048]{2,0,1:T(2,128)(2,1)}), bf16[2,768,2048]{2,0,1:T(2,128)(2,1)}, u32[]{:S(2)}, u32[]{:S(2)}) async-start(bf16[2,768,2048]{2,0,1:T(2,128)(2,1)} %copy.115), calls=%async_computation.1 | async-start | bytes 12582912 | tf_op jit(solution)/shard_map/all_to_all | solution.py:164
  177.6 230.5 %all-gather.19.cloned.1.call-start = ((), (), s32[]{:S(2)}) async-start(), calls=%async_computation.7 | async-start | bytes 8912896 | tf_op jit(solution)/shard_map/all_gather | solution.py:16
  178.0 115.9 %copy-start.32 = (pred[128,128]{1,0:T(8,128)(4,1)}, pred[128,128]{1,0:T(8,128)(4,1)S(1)}, u32[]{:S(2)}) copy-start(pred[128,128]{1,0:T(8,128)(4,1)S(1)} %get-tuple-element.234) | copy-start | bytes 49156
  268.0 1.0 copy-start.13
  269.1 1.4 copy-start.35
  269.1 1.8 copy-start.41
  270.5 9.2 %copy-start.29 = (bf16[128,2048]{1,0:T(8,128)(2,1)}, bf16[128,2048]{1,0:T(8,128)(2,1)S(1)}, u32[]{:S(2)}) copy-start(bf16[128,2048]{1,0:T(8,128)(2,1)S(1)} %get-tuple-element.227) | copy-start | bytes 1572868
  279.7 10.8 %collective-permute-start = (bf16[3,4096]{1,0:T(4,128)(2,1)S(1)}, bf16[3,4096]{1,0:T(4,128)(2,1)S(1)}, u32[]{:S(2)}, u32[]{:S(2)}) collective-permute-start(bf16[3,4096]{1,0:T(4,128)(2,1)S(1)} %slice.199), channel_id=1, source_target_pairs={{0,1},{1,2},{2,3},{3,4},{4,5},{5,6},{6,7},{7,8},{8,9},{9,10},{10,1... | collective-permute-start | bytes 73736 | tf_op jit(solution)/shard_map/ppermute | solution.py:10
  292.0 1.6 copy-start.10
  293.9 3.1 copy-start.2
  296.5 0.8 copy-start.16
  296.7 0.8 copy-start.18
  296.7 1.0 copy-start.20
  297.0 0.9 copy-start.22
  297.0 1.1 copy-start.24
  297.7 19.1 %copy-start.26 = (f32[1,2,2,2,16,8,8]{6,5,4,3,2,1,0:T(8,128)}, f32[1,2,2,2,16,8,8]{6,5,4,3,2,1,0:T(8,128)S(1)}, u32[]{:S(2)}) copy-start(f32[1,2,2,2,16,8,8]{6,5,4,3,2,1,0:T(8,128)S(1)} %get-tuple-element.201) | copy-start | bytes 98308
  297.8 19.1 %copy-start.27 = (f32[1,2,2,2,16,8,8]{6,5,4,3,2,1,0:T(8,128)}, f32[1,2,2,2,16,8,8]{6,5,4,3,2,1,0:T(8,128)S(1)}, u32[]{:S(2)}) copy-start(f32[1,2,2,2,16,8,8]{6,5,4,3,2,1,0:T(8,128)S(1)} %get-tuple-element.202) | copy-start | bytes 98308
  307.3 9.5 %copy-start.30 = (f32[1,2,2,2,2,2,16,2,2]{8,7,6,5,4,3,2,1,0:T(2,128)S(1)}, f32[1,2,2,2,2,2,16,2,2]{8,7,6,5,4,3,2,1,0:T(2,128)}, u32[]{:S(2)}) copy-start(f32[1,2,2,2,2,2,16,2,2]{8,7,6,5,4,3,2,1,0:T(2,128)} %copy.134) | copy-start | bytes 24580
  307.3 9.5 %copy-start.31 = (f32[1,2,2,2,2,2,16,2,2]{8,7,6,5,4,3,2,1,0:T(2,128)S(1)}, f32[1,2,2,2,2,2,16,2,2]{8,7,6,5,4,3,2,1,0:T(2,128)}, u32[]{:S(2)}) copy-start(f32[1,2,2,2,2,2,16,2,2]{8,7,6,5,4,3,2,1,0:T(2,128)} %copy.135) | copy-start | bytes 24580
  317.8 5.5 copy-start.23
  317.8 5.5 copy-start.25
  323.3 2.3 copy-start.19
  323.3 2.3 copy-start.21
  325.6 1.6 copy-start.17
  328.9 1.7 copy-start.37
  328.9 1.7 copy-start.38
  329.1 3.0 copy-start.11
  329.9 6.6 copy-start.14
  329.9 6.6 copy-start.15
  332.1 4.4 copy-start.39
  333.4 8.9 %copy-start.6 = (f32[16,128,128]{2,1,0:T(8,128)}, f32[16,128,128]{2,1,0:T(8,128)S(1)}, u32[]{:S(2)}) copy-start(f32[16,128,128]{2,1,0:T(8,128)S(1)} %fusion.45) | copy-start | bytes 3145732
  336.5 144.2 %all-gather.17.cloned.1.call-start = ((), (), s32[]{:S(2)}) async-start(), calls=%async_computation.6 | async-start | bytes 8912896 | tf_op jit(solution)/shard_map/all_gather | solution.py:16
  339.5 2.9 copy-start.8
  342.4 310.3 %all-gather.11.cloned.1.call-start = ((), (), s32[]{:S(2)}) async-start(), calls=%async_computation.3 | async-start | bytes 17825792 | tf_op jit(solution)/shard_map/all_gather | solution.py:43
  485.8 209.9 %all-gather.13.cloned.1.call-start = ((), (), s32[]{:S(2)}) async-start(), calls=%async_computation.4 | async-start | bytes 4718592 | tf_op jit(solution)/shard_map/all_gather | solution.py:49
  662.0 4.6 copy-start.33
  663.1 66.4 %all-gather.15.cloned.1.call-start = ((), (), s32[]{:S(2)}) async-start(), calls=%async_computation.5 | async-start | bytes 4718592 | tf_op jit(solution)/shard_map/all_gather | solution.py:49
  663.6 2.9 copy-start.3
  665.5 1.0 copy-start.4
  742.1 1.2 copy-start.7
  742.1 1.5 copy-start.9
  742.1 2.7 copy-start.5
  742.1 2.7 copy-start.36
  743.6 3.1 copy-start.28
  744.8 3.9 copy-start.42
  744.9 5.1 copy-start.1
Sparse Core Ops, SparseCore 0:
  10.1 225.6 all-gather.8
  336.6 71.4 all-gather.18
  410.3 70.3 all-gather.16
  485.9 166.7 all-gather.10
  663.2 32.4 all-gather.12
  697.3 32.1 all-gather.14
